TPU v7x, 32 devices: a whole 2x2x4 slice. The times are simulated.
32 devices in a mesh: wide: 8 (over z, y), fields: 4 (over x, core).
Axes of the slice: x: 2, y: 2, z: 4, core: 2. Of those that a mesh axis runs over, the one named last changes fastest.
Arguments:
- vectors: float32 [256, 16384], P('wide', 'fields'), may hold values from 0.03 to 82, as said below
- pivot_ids: int32 [8], replicated, may hold values from 0 to 255
Outputs:
- similarity: float32 [256, 4, 256], P('wide', None, 'fields')
Inputs may be any that keep to these rules, and one draw needn't show every extreme that they name: `vectors`: every entry is positive.
All inputs are finite; a program needn't handle non-finite values.
Results may differ from a plain program's by a relative error of at most 0.0003.
Values sent between devices are 32-bit elements; how exact they have to be, the bound alone decides.
A program may use at most 64 MiB of HBM per device.

v0:
```python
import jax
import jax.numpy as jnp
from jax import lax
from jax.sharding import PartitionSpec as P

STEPS = 4


def from_behind(value, axis, steps):
    count = lax.axis_size(axis)
    pairs = [(source, (source + steps) % count) for source in range(count)]
    return lax.ppermute(value, axis, pairs)


def triple_table(owned, pivots, minima, partner):
    with_pivot = jnp.sum(minima, axis=-1)
    pivot_side = jnp.sum(jnp.minimum(pivots[:, None, :], partner[None, :, :]), axis=-1)
    pair_side = jnp.sum(jnp.minimum(owned[:, None, :], partner[None, :, :]), axis=-1)
    triple = lax.map(
        lambda layer: jnp.sum(jnp.minimum(layer[:, None, :], partner[None, :, :]), axis=-1),
        jnp.transpose(minima, (1, 0, 2)),
    )
    return (
        with_pivot[:, :, None]
        + pivot_side[None, :, :]
        + pair_side[:, None, :]
        - jnp.transpose(triple, (1, 0, 2))
    )


def body(vectors, pivot_ids):
    row_count = vectors.shape[0]
    pivot_count = pivot_ids.shape[0]
    first_row = lax.axis_index("wide") * row_count
    chosen = (
        pivot_ids[:, None] == first_row + jnp.arange(row_count, dtype=jnp.int32)[None, :]
    ).astype(jnp.float32)
    pivot_part = jnp.dot(
        chosen, vectors, precision=lax.Precision.HIGHEST, preferred_element_type=jnp.float32
    )
    pivots = lax.psum(pivot_part, "wide")
    owned_total, pivot_total = lax.psum(
        (jnp.sum(vectors, axis=1), jnp.sum(pivots, axis=1)), "fields"
    )
    minima = jnp.minimum(vectors[:, None, :], pivots[None, :, :])
    partner, partner_total = (vectors, owned_total)
    numerators = []
    partner_totals = []
    for stride in range(1, STEPS + 1):
        partner, partner_total = from_behind((partner, partner_total), "wide", 1)
        partner_totals.append(partner_total)
        numerator = triple_table(vectors, pivots, minima, partner).reshape(
            row_count, pivot_count * row_count
        )
        numerators.append(numerator)
    stacked = jnp.stack(numerators, axis=1)
    shares = lax.psum_scatter(stacked, "fields", scatter_dimension=2, tiled=True)
    share_width = shares.shape[2]
    offset = lax.axis_index("fields") * share_width
    step_totals = jnp.stack(partner_totals, axis=0)
    denominator = (
        owned_total[:, None, None, None]
        + pivot_total[None, None, :, None]
        + step_totals[None, :, None, :]
    )
    denominator = denominator.reshape(row_count, STEPS, pivot_count * row_count)
    denominator = lax.dynamic_slice_in_dim(denominator, offset, share_width, 2)
    return 1.5 * shares / denominator


def solution(mesh):
    placed = (P("wide", "fields"), P())
    return jax.shard_map(
        body, mesh=mesh, in_specs=placed, out_specs=P("wide", None, "fields"), check_vma=False
    )
```

profile of v0, /device:TPU:0, one launch (start us, length us, event | category | flops | bytes accessed | tf_op | source)
XLA Modules:
  0.0 292.2 jit_solution(9529471152527923765)
XLA Ops:
  6.5 3.0 %collective-permute-start = (f32[32,4096]{1,0:T(8,128)}, f32[32,4096]{1,0:T(8,128)S(1)}, u32[]{:S(2)}, u32[]{:S(2)}) collective-permute-start(f32[32,4096]{1,0:T(8,128)} %param.10), channel_id=1, source_target_pairs={{0,4},{4,8},{8,12},{12,16},{16,20},{20,24},{24,28},{28,0},{1,5},{5... | collective-permute-start | bytes 1572872 | tf_op jit(solution)/shard_map/ppermute | solution.py:12
  9.5 15.2 %collective-permute-done = f32[32,4096]{1,0:T(8,128)S(1)} collective-permute-done((f32[32,4096]{1,0:T(8,128)}, f32[32,4096]{1,0:T(8,128)S(1)}, u32[]{:S(2)}, u32[]{:S(2)}) %collective-permute-start) | collective-permute-done | bytes 524320 | tf_op jit(solution)/shard_map/ppermute | solution.py:12
  24.7 15.8 %collective-permute-done.1 = f32[32,4096]{1,0:T(8,128)S(1)} collective-permute-done((f32[32,4096]{1,0:T(8,128)S(1)}, f32[32,4096]{1,0:T(8,128)S(1)}, u32[]{:S(2)}, u32[]{:S(2)}) %collective-permute-start.1) | collective-permute-done | bytes 524320 | tf_op jit(solution)/shard_map/ppermute | solution.py:12
  42.6 13.3 %collective-permute-done.2 = f32[32,4096]{1,0:T(8,128)S(1)} collective-permute-done((f32[32,4096]{1,0:T(8,128)S(1)}, f32[32,4096]{1,0:T(8,128)S(1)}, u32[]{:S(2)}, u32[]{:S(2)}) %collective-permute-start.2) | collective-permute-done | bytes 524320 | tf_op jit(solution)/shard_map/ppermute | solution.py:12
  57.0 65.4 %all-reduce.3.cloned.1.call-done = f32[8,4096]{1,0:T(8,128)} async-done(((f32[8,4096]{1,0:T(8,128)}), f32[8,4096]{1,0:T(8,128)}) %all-reduce.3.cloned.1.call-update) | async-done | bytes 131088 | tf_op jit(solution)/shard_map/psum | solution.py:41
  123.4 5.7 %all-reduce = (f32[32]{0:T(128)S(1)}, f32[8]{0:T(128)S(1)}) all-reduce(f32[32]{0:T(128)S(1)} %reduce_sum.156, f32[8]{0:T(128)S(1)} %reduce_sum.157), channel_id=1, replica_groups=mesh['wide'=8,'fields'=4] {'fields'}, use_global_device_ids=true, to_apply=%region_24.25 | all-reduce | flops 40 | bytes 320 | tf_op jit(solution)/shard_map/psum | solution.py:42
  129.8 5.6 %collective-permute-done.4 = f32[32]{0:T(128)S(1)} collective-permute-done((f32[32]{0:T(128)S(1)}, f32[32]{0:T(128)S(1)}, u32[]{:S(2)}, u32[]{:S(2)}) %collective-permute-start.4) | collective-permute-done | bytes 160 | tf_op jit(solution)/shard_map/ppermute | solution.py:12
  137.0 4.7 %collective-permute-done.5 = f32[32]{0:T(128)S(1)} collective-permute-done((f32[32]{0:T(128)S(1)}, f32[32]{0:T(128)S(1)}, u32[]{:S(2)}, u32[]{:S(2)}) %collective-permute-start.5) | collective-permute-done | bytes 160 | tf_op jit(solution)/shard_map/ppermute | solution.py:12
  141.9 6.1 %collective-permute-done.6 = f32[32]{0:T(128)S(1)} collective-permute-done((f32[32]{0:T(128)S(1)}, f32[32]{0:T(128)S(1)}, u32[]{:S(2)}, u32[]{:S(2)}) %collective-permute-start.6) | collective-permute-done | bytes 160 | tf_op jit(solution)/shard_map/ppermute | solution.py:12
  147.9 5.3 %minimum_reduce_fusion.11 = (f32[8,32]{1,0:T(8,128)S(1)}, f32[8,32]{1,0:T(8,128)S(1)}, f32[8,32]{1,0:T(8,128)S(1)}, f32[8,32]{1,0:T(8,128)S(1)}, f32[8,32,4096]{2,1,0:T(8,128)}) fusion(f32[32,4096]{1,0:T(8,128)S(1)} %collective-permute-done, f32[8,4096]{1,0:T(8,128)} %all-reduce.3.cloned.1.call-done, f32[32,4096]{1,0:T(8,128)S(1)} %collective-permute-done.1, ...), kind=kLoop, calls=%fused_computation.19 | loop fusion | flops 9436160 | bytes 6950912 | tf_op jit(solution)/shard_map/reduce_sum | solution.py:17
  153.2 25.6 %while.40 = (s32[]{:T(128)}, f32[8,32,32]{2,1,0:T(8,128)S(1)}, f32[8,32,4096]{2,1,0:T(8,128)}, f32[32,4096]{1,0:T(8,128)S(1)}, s32[]{:T(128)}) while((s32[]{:T(128)}, f32[8,32,32]{2,1,0:T(8,128)S(1)}, f32[8,32,4096]{2,1,0:T(8,128)}, f32[32,4096]{1,0:T(8,128)S(1)}, s32[]{:T(128)}) %tuple.67), condition=%wide.region_6.0_spmd, body=%wide.region_4.6_spmd.sunk | while | flops 8387586 | bytes 2134093 | solution.py:19
  154.5 2.1 minimum_reduce_fusion.17
  157.7 2.1 minimum_reduce_fusion.17
  160.8 2.1 minimum_reduce_fusion.17
  178.9 25.4 %while.41 = (s32[]{:T(128)}, f32[8,32,32]{2,1,0:T(8,128)S(1)}, f32[8,32,4096]{2,1,0:T(8,128)}, f32[32,4096]{1,0:T(8,128)S(1)}, s32[]{:T(128)}) while((s32[]{:T(128)}, f32[8,32,32]{2,1,0:T(8,128)S(1)}, f32[8,32,4096]{2,1,0:T(8,128)}, f32[32,4096]{1,0:T(8,128)S(1)}, s32[]{:T(128)}) %tuple.83), condition=%wide.region_11.12_spmd, body=%wide.region_9.11_spmd.sunk | while | flops 8387586 | bytes 2134093 | solution.py:19
  202.2 2.1 minimum_reduce_fusion.18
  204.3 25.4 %while.42 = (s32[]{:T(128)}, f32[8,32,32]{2,1,0:T(8,128)S(1)}, f32[8,32,4096]{2,1,0:T(8,128)}, f32[32,4096]{1,0:T(8,128)S(1)}, s32[]{:T(128)}) while((s32[]{:T(128)}, f32[8,32,32]{2,1,0:T(8,128)S(1)}, f32[8,32,4096]{2,1,0:T(8,128)}, f32[32,4096]{1,0:T(8,128)S(1)}, s32[]{:T(128)}) %tuple.84), condition=%wide.region_16.17_spmd, body=%wide.region_14.16_spmd.sunk | while | flops 8387586 | bytes 2134093 | solution.py:19
  224.5 2.1 minimum_reduce_fusion.19
  229.8 25.5 %while.43 = (s32[]{:T(128)}, f32[8,32,32]{2,1,0:T(8,128)S(1)}, f32[8,32,4096]{2,1,0:T(8,128)}, f32[32,4096]{1,0:T(8,128)S(1)}, s32[]{:T(128)}) while((s32[]{:T(128)}, f32[8,32,32]{2,1,0:T(8,128)S(1)}, f32[8,32,4096]{2,1,0:T(8,128)}, f32[32,4096]{1,0:T(8,128)S(1)}, s32[]{:T(128)}) %tuple.85), condition=%wide.region_21.22_spmd, body=%wide.region_19.21_spmd.sunk | while | flops 8387586 | bytes 2134093 | solution.py:19
  234.1 2.1 minimum_reduce_fusion.20
  243.6 2.1 minimum_reduce_fusion.20
  253.2 2.1 minimum_reduce_fusion.20
  255.3 4.9 %minimum_reduce_fusion.7 = (f32[32,32]{1,0:T(8,128)S(1)}, f32[32,32]{1,0:T(8,128)S(1)}, f32[32,32]{1,0:T(8,128)S(1)}, f32[32,32]{1,0:T(8,128)S(1)}) fusion(f32[32,4096]{1,0:T(8,128)S(1)} %get-tuple-element.311, f32[32,4096]{1,0:T(8,128)S(1)} %copy-done, f32[32,4096]{1,0:T(8,128)S(1)} %get-tuple-element.314, f32[32,4096]{1,0:T(8,128)S(1)} %get-tuple-element.317, ...), kind=kLoop, calls=%fused_computation.15 | loop fusion | flops 33550336 | bytes 2637824 | tf_op jit(solution)/shard_map/reduce_sum | solution.py:18
  262.6 21.2 %reduce-scatter.4.cloned.1.call-done = f32[64,128]{1,0:T(8,128)} async-done(((f32[256,128]{1,0:T(8,128)}), f32[64,128]{1,0:T(8,128)}) %reduce-scatter.4.cloned.1.call-update) | async-done | bytes 32784
  (137 shorter events, 95.6 us)
Async XLA Ops:
  6.5 115.9 %all-reduce.3.cloned.1.call-start = ((), (), s32[]{:S(2)}) async-start(), calls=%async_computation.1 | async-start | bytes 262144 | tf_op jit(solution)/shard_map/psum | solution.py:41
  6.5 18.2 %collective-permute-start = (f32[32,4096]{1,0:T(8,128)}, f32[32,4096]{1,0:T(8,128)S(1)}, u32[]{:S(2)}, u32[]{:S(2)}) collective-permute-start(f32[32,4096]{1,0:T(8,128)} %param.10), channel_id=1, source_target_pairs={{0,4},{4,8},{8,12},{12,16},{16,20},{20,24},{24,28},{28,0},{1,5},{5... | collective-permute-start | bytes 1572872 | tf_op jit(solution)/shard_map/ppermute | solution.py:12
  24.7 15.8 %collective-permute-start.1 = (f32[32,4096]{1,0:T(8,128)S(1)}, f32[32,4096]{1,0:T(8,128)S(1)}, u32[]{:S(2)}, u32[]{:S(2)}) collective-permute-start(f32[32,4096]{1,0:T(8,128)S(1)} %collective-permute-done), channel_id=1, source_target_pairs={{0,4},{4,8},{8,12},{12,16},{16,20},{20,24},{24,28},{28,0},{1,5},{5... | collective-permute-start | bytes 1572872 | tf_op jit(solution)/shard_map/ppermute | solution.py:12
  40.5 15.3 %collective-permute-start.2 = (f32[32,4096]{1,0:T(8,128)S(1)}, f32[32,4096]{1,0:T(8,128)S(1)}, u32[]{:S(2)}, u32[]{:S(2)}) collective-permute-start(f32[32,4096]{1,0:T(8,128)S(1)} %collective-permute-done.1), channel_id=1, source_target_pairs={{0,4},{4,8},{8,12},{12,16},{16,20},{20,24},{24,28},{28,0},{1,5},{5... | collective-permute-start | bytes 1572872 | tf_op jit(solution)/shard_map/ppermute | solution.py:12
  42.5 241.2 %reduce-scatter.4.cloned.1.call-start = ((), (), s32[]{:S(2)}) async-start(), calls=%async_computation.2 | async-start | bytes 163840
  55.8 92.1 %collective-permute-start.3 = (f32[32,4096]{1,0:T(8,128)S(1)}, f32[32,4096]{1,0:T(8,128)S(1)}, u32[]{:S(2)}, u32[]{:S(2)}) collective-permute-start(f32[32,4096]{1,0:T(8,128)S(1)} %collective-permute-done.2), channel_id=1, source_target_pairs={{0,4},{4,8},{8,12},{12,16},{16,20},{20,24},{24,28},{28,0},{1,5},{5... | collective-permute-start | bytes 1572872 | tf_op jit(solution)/shard_map/ppermute | solution.py:12
  129.1 6.3 %collective-permute-start.4 = (f32[32]{0:T(128)S(1)}, f32[32]{0:T(128)S(1)}, u32[]{:S(2)}, u32[]{:S(2)}) collective-permute-start(f32[32]{0:T(128)S(1)} %get-tuple-element.137), channel_id=1, source_target_pairs={{0,4},{4,8},{8,12},{12,16},{16,20},{20,24},{24,28},{28,0},{1,5},{5... | collective-permute-start | bytes 392 | tf_op jit(solution)/shard_map/ppermute | solution.py:12
  135.4 6.3 %collective-permute-start.5 = (f32[32]{0:T(128)S(1)}, f32[32]{0:T(128)S(1)}, u32[]{:S(2)}, u32[]{:S(2)}) collective-permute-start(f32[32]{0:T(128)S(1)} %collective-permute-done.4), channel_id=1, source_target_pairs={{0,4},{4,8},{8,12},{12,16},{16,20},{20,24},{24,28},{28,0},{1,5},{5... | collective-permute-start | bytes 392 | tf_op jit(solution)/shard_map/ppermute | solution.py:12
  141.7 6.3 %collective-permute-start.6 = (f32[32]{0:T(128)S(1)}, f32[32]{0:T(128)S(1)}, u32[]{:S(2)}, u32[]{:S(2)}) collective-permute-start(f32[32]{0:T(128)S(1)} %collective-permute-done.5), channel_id=1, source_target_pairs={{0,4},{4,8},{8,12},{12,16},{16,20},{20,24},{24,28},{28,0},{1,5},{5... | collective-permute-start | bytes 392 | tf_op jit(solution)/shard_map/ppermute | solution.py:12
  147.9 114.4 %collective-permute-start.7 = (f32[32]{0:T(128)S(1)}, f32[32]{0:T(128)S(1)}, u32[]{:S(2)}, u32[]{:S(2)}) collective-permute-start(f32[32]{0:T(128)S(1)} %collective-permute-done.6), channel_id=1, source_target_pairs={{0,4},{4,8},{8,12},{12,16},{16,20},{20,24},{24,28},{28,0},{1,5},{5... | collective-permute-start | bytes 392 | tf_op jit(solution)/shard_map/ppermute | solution.py:12
  229.8 25.5 %copy-start = (f32[32,4096]{1,0:T(8,128)S(1)}, f32[32,4096]{1,0:T(8,128)}, u32[]{:S(2)}) copy-start(f32[32,4096]{1,0:T(8,128)} %param.10) | copy-start | bytes 1572868
Sparse Core Ops, SparseCore 0:
  42.6 79.7 all-reduce.2
  262.4 21.2 reduce-scatter.3
where the time goes:
time: 294 us; the launch traced here: 292 us
  waiting for transfers between devices  147 us (50%)
  other arithmetic  80.9 us (28%)
  local copies, waits for them, and re-layouts  38.8 us (13%)
  between operations  13.6 us (5%)
  blocking collectives  5.66 us (2%)
  starting transfers between devices  3.69 us (1%)
    reduce_sum x32, other arithmetic, triple_table(): jnp.sum(jnp.minimum(layer[:, None, :], partner[None, :, :]), axis=-1)  66.7 us
    psum x1, waiting for transfers between devices, body(): pivots = lax.psum(pivot_part, 'wide')  65.4 us
    ppermute x8, waiting for transfers between devices, from_behind(): return lax.ppermute(value, axis, pairs)  60.6 us
    min x32, local copies, waits for them, and re-layouts, triple_table(): jnp.minimum(layer[:, None, :], partner[None, :, :])  34.6 us
    unnamed x3, waiting for transfers between devices  21.2 us
  transfers between devices with their start and end apart: 10, of which 8 were waited for; matrix products, arithmetic and copies ran while one was open for 41% of the time, Pallas kernels for 0%

commit v1 on v0

--- a/solution.py
+++ b/solution.py
@@ -38,7 +38,8 @@
     pivot_part = jnp.dot(
         chosen, vectors, precision=lax.Precision.HIGHEST, preferred_element_type=jnp.float32
     )
-    pivots = lax.psum(pivot_part, "wide")
+    parts = lax.all_gather(pivot_part, "wide", axis=0, tiled=False)
+    pivots = parts.sum(axis=0)
     owned_total, pivot_total = lax.psum(
         (jnp.sum(vectors, axis=1), jnp.sum(pivots, axis=1)), "fields"
     )

time: 294 us -> 245 us (0.83)
  waiting for transfers between devices: 147 us -> 84.5 us
  starting transfers between devices: 3.69 us -> 16.7 us
    psum x1 -> x0, waiting for transfers between devices: 65.4 us -> none  [body(): pivots = lax.psum(pivot_part, 'wide')]
    ppermute x8, starting transfers between devices: 3.65 us -> 16.7 us  [from_behind(): return lax.ppermute(value, axis, pairs)]
  transfers between devices with their start and end apart: 10 -> 10, of which waited for: 8 -> 7; matrix products, arithmetic and copies ran while one was open for 41% -> 49% of each run, Pallas kernels for 0% -> 0%
where the time goes in v1:
time: 245 us; the launch traced here: 243 us
  waiting for transfers between devices  84.5 us (34%)
  other arithmetic  81.4 us (33%)
  local copies, waits for them, and re-layouts  38.8 us (16%)
  starting transfers between devices  16.7 us (7%)
  between operations  13.6 us (6%)
  blocking collectives  5.96 us (2%)
    reduce_sum x32, other arithmetic, triple_table(): jnp.sum(jnp.minimum(layer[:, None, :], partner[None, :, :]), axis=-1)  66.7 us
    ppermute x8, waiting for transfers between devices, from_behind(): return lax.ppermute(value, axis, pairs)  61.6 us
    min x32, local copies, waits for them, and re-layouts, triple_table(): jnp.minimum(layer[:, None, :], partner[None, :, :])  34.6 us
    unnamed x3, waiting for transfers between devices  21.2 us
    ppermute x8, starting transfers between devices, from_behind(): return lax.ppermute(value, axis, pairs)  16.7 us
    psum x1, blocking collectives, body(): lax.psum((jnp.sum(vectors, axis=1), jnp.sum(pivots, axis=1)), 'fields')  5.96 us
    reduce_sum x1, other arithmetic, triple_table(): jnp.sum(jnp.minimum(owned[:, None, :], partner[None, :, :]), axis=-1)  4.93 us
  transfers between devices with their start and end apart: 10, of which 7 were waited for; matrix products, arithmetic and copies ran while one was open for 49% of the time, Pallas kernels for 0%

profile of v1, /device:TPU:0, one launch (start us, length us, event | category | flops | bytes accessed | tf_op | source)
XLA Modules:
  0.0 243.4 jit_solution(17380839896470327873)
XLA Ops:
  8.7 3.0 %collective-permute-start = (f32[32,4096]{1,0:T(8,128)}, f32[32,4096]{1,0:T(8,128)S(1)}, u32[]{:S(2)}, u32[]{:S(2)}) collective-permute-start(f32[32,4096]{1,0:T(8,128)} %param.10), channel_id=1, source_target_pairs={{0,4},{4,8},{8,12},{12,16},{16,20},{20,24},{24,28},{28,0},{1,5},{5... | collective-permute-start | bytes 1572872 | tf_op jit(solution)/shard_map/ppermute | solution.py:12
  11.7 16.8 %collective-permute-done = f32[32,4096]{1,0:T(8,128)S(1)} collective-permute-done((f32[32,4096]{1,0:T(8,128)}, f32[32,4096]{1,0:T(8,128)S(1)}, u32[]{:S(2)}, u32[]{:S(2)}) %collective-permute-start) | collective-permute-done | bytes 524320 | tf_op jit(solution)/shard_map/ppermute | solution.py:12
  28.5 15.4 %collective-permute-done.1 = f32[32,4096]{1,0:T(8,128)S(1)} collective-permute-done((f32[32,4096]{1,0:T(8,128)S(1)}, f32[32,4096]{1,0:T(8,128)S(1)}, u32[]{:S(2)}, u32[]{:S(2)}) %collective-permute-start.1) | collective-permute-done | bytes 524320 | tf_op jit(solution)/shard_map/ppermute | solution.py:12
  45.1 20.7 %collective-permute-done.2 = f32[32,4096]{1,0:T(8,128)S(1)} collective-permute-done((f32[32,4096]{1,0:T(8,128)S(1)}, f32[32,4096]{1,0:T(8,128)S(1)}, u32[]{:S(2)}, u32[]{:S(2)}) %collective-permute-start.2) | collective-permute-done | bytes 524320 | tf_op jit(solution)/shard_map/ppermute | solution.py:12
  68.9 6.0 %all-reduce = (f32[32]{0:T(128)S(1)}, f32[8]{0:T(128)S(1)}) all-reduce(f32[32]{0:T(128)S(1)} %reduce_sum.166, f32[8]{0:T(128)S(1)} %reduce_sum.167), channel_id=1, replica_groups=mesh['wide'=8,'fields'=4] {'fields'}, use_global_device_ids=true, to_apply=%region_24.25 | all-reduce | flops 40 | bytes 320 | tf_op jit(solution)/shard_map/psum | solution.py:43
  74.9 11.4 %collective-permute-start.4 = (f32[32]{0:T(128)S(1)}, f32[32]{0:T(128)S(1)}, u32[]{:S(2)}, u32[]{:S(2)}) collective-permute-start(f32[32]{0:T(128)S(1)} %get-tuple-element.137), channel_id=1, source_target_pairs={{0,4},{4,8},{8,12},{12,16},{16,20},{20,24},{24,28},{28,0},{1,5},{5... | collective-permute-start | bytes 392 | tf_op jit(solution)/shard_map/ppermute | solution.py:12
  87.7 2.2 collective-permute-start.5
  91.4 2.6 %collective-permute-done.5 = f32[32]{0:T(128)S(1)} collective-permute-done((f32[32]{0:T(128)S(1)}, f32[32]{0:T(128)S(1)}, u32[]{:S(2)}, u32[]{:S(2)}) %collective-permute-start.5) | collective-permute-done | bytes 160 | tf_op jit(solution)/shard_map/ppermute | solution.py:12
  94.2 6.1 %collective-permute-done.6 = f32[32]{0:T(128)S(1)} collective-permute-done((f32[32]{0:T(128)S(1)}, f32[32]{0:T(128)S(1)}, u32[]{:S(2)}, u32[]{:S(2)}) %collective-permute-start.6) | collective-permute-done | bytes 160 | tf_op jit(solution)/shard_map/ppermute | solution.py:12
  100.3 4.1 %minimum_reduce_fusion.11 = (f32[8,32]{1,0:T(8,128)S(1)}, f32[8,32]{1,0:T(8,128)S(1)}, f32[8,32]{1,0:T(8,128)S(1)}, f32[8,32]{1,0:T(8,128)S(1)}, f32[8,32,4096]{2,1,0:T(8,128)}) fusion(f32[32,4096]{1,0:T(8,128)S(1)} %collective-permute-done, f32[8,4096]{1,0:T(8,128)S(1)} %bitcast_reduce_fusion, f32[32,4096]{1,0:T(8,128)S(1)} %collective-permute-done.1, ...), kind=kLoop, calls=%fused_computation.19 | loop fusion | flops 9436160 | bytes 6950912 | tf_op jit(solution)/shard_map/reduce_sum | solution.py:17
  104.5 25.6 %while.43 = (s32[]{:T(128)}, f32[8,32,32]{2,1,0:T(8,128)S(1)}, f32[8,32,4096]{2,1,0:T(8,128)}, f32[32,4096]{1,0:T(8,128)S(1)}, s32[]{:T(128)}) while((s32[]{:T(128)}, f32[8,32,32]{2,1,0:T(8,128)S(1)}, f32[8,32,4096]{2,1,0:T(8,128)}, f32[32,4096]{1,0:T(8,128)S(1)}, s32[]{:T(128)}) %tuple.76), condition=%wide.region_21.22_spmd, body=%wide.region_19.21_spmd.sunk | while | flops 8387586 | bytes 2134093 | solution.py:19
  105.7 2.1 minimum_reduce_fusion.20
  108.9 2.1 minimum_reduce_fusion.20
  112.1 2.1 minimum_reduce_fusion.20
  115.3 2.1 minimum_reduce_fusion.20
  128.0 2.1 minimum_reduce_fusion.20
  130.1 25.4 %while.42 = (s32[]{:T(128)}, f32[8,32,32]{2,1,0:T(8,128)S(1)}, f32[8,32,4096]{2,1,0:T(8,128)}, f32[32,4096]{1,0:T(8,128)S(1)}, s32[]{:T(128)}) while((s32[]{:T(128)}, f32[8,32,32]{2,1,0:T(8,128)S(1)}, f32[8,32,4096]{2,1,0:T(8,128)}, f32[32,4096]{1,0:T(8,128)S(1)}, s32[]{:T(128)}) %tuple.83), condition=%wide.region_16.17_spmd, body=%wide.region_14.16_spmd.sunk | while | flops 8387586 | bytes 2134093 | solution.py:19
  131.2 2.1 minimum_reduce_fusion.19
  134.4 2.1 minimum_reduce_fusion.19
  155.5 25.4 %while.41 = (s32[]{:T(128)}, f32[8,32,32]{2,1,0:T(8,128)S(1)}, f32[8,32,4096]{2,1,0:T(8,128)}, f32[32,4096]{1,0:T(8,128)S(1)}, s32[]{:T(128)}) while((s32[]{:T(128)}, f32[8,32,32]{2,1,0:T(8,128)S(1)}, f32[8,32,4096]{2,1,0:T(8,128)}, f32[32,4096]{1,0:T(8,128)S(1)}, s32[]{:T(128)}) %tuple.84), condition=%wide.region_11.12_spmd, body=%wide.region_9.11_spmd.sunk | while | flops 8387586 | bytes 2134093 | solution.py:19
  181.0 25.4 %while.40 = (s32[]{:T(128)}, f32[8,32,32]{2,1,0:T(8,128)S(1)}, f32[8,32,4096]{2,1,0:T(8,128)}, f32[32,4096]{1,0:T(8,128)S(1)}, s32[]{:T(128)}) while((s32[]{:T(128)}, f32[8,32,32]{2,1,0:T(8,128)S(1)}, f32[8,32,4096]{2,1,0:T(8,128)}, f32[32,4096]{1,0:T(8,128)S(1)}, s32[]{:T(128)}) %tuple.85), condition=%wide.region_6.0_spmd, body=%wide.region_4.6_spmd.sunk | while | flops 8387586 | bytes 2134093 | solution.py:19
  204.3 2.1 minimum_reduce_fusion.17
  206.4 4.9 %minimum_reduce_fusion.7 = (f32[32,32]{1,0:T(8,128)S(1)}, f32[32,32]{1,0:T(8,128)S(1)}, f32[32,32]{1,0:T(8,128)S(1)}, f32[32,32]{1,0:T(8,128)S(1)}) fusion(f32[32,4096]{1,0:T(8,128)S(1)} %get-tuple-element.311, f32[32,4096]{1,0:T(8,128)S(1)} %copy-done, f32[32,4096]{1,0:T(8,128)S(1)} %get-tuple-element.314, f32[32,4096]{1,0:T(8,128)S(1)} %get-tuple-element.317, ...), kind=kLoop, calls=%fused_computation.15 | loop fusion | flops 33550336 | bytes 2637824 | tf_op jit(solution)/shard_map/reduce_sum | solution.py:18
  213.7 21.2 %reduce-scatter.4.cloned.1.call-done = f32[64,128]{1,0:T(8,128)} async-done(((f32[256,128]{1,0:T(8,128)}), f32[64,128]{1,0:T(8,128)}) %reduce-scatter.4.cloned.1.call-update) | async-done | bytes 32784
  (140 shorter events, 98.2 us)
Async XLA Ops:
  6.5 93.8 %copy-start = (f32[32,4096]{1,0:T(8,128)S(1)}, f32[32,4096]{1,0:T(8,128)}, u32[]{:S(2)}) copy-start(f32[32,4096]{1,0:T(8,128)} %param.10) | copy-start | bytes 1572868
  6.5 60.9 %all-gather.3.cloned.1.call-start = ((), (), s32[]{:S(2)}) async-start(), calls=%async_computation.1 | async-start | bytes 1179648 | tf_op jit(solution)/shard_map/all_gather | solution.py:41
  8.6 226.3 %reduce-scatter.4.cloned.1.call-start = ((), (), s32[]{:S(2)}) async-start(), calls=%async_computation.2 | async-start | bytes 163840
  8.7 19.8 %collective-permute-start = (f32[32,4096]{1,0:T(8,128)}, f32[32,4096]{1,0:T(8,128)S(1)}, u32[]{:S(2)}, u32[]{:S(2)}) collective-permute-start(f32[32,4096]{1,0:T(8,128)} %param.10), channel_id=1, source_target_pairs={{0,4},{4,8},{8,12},{12,16},{16,20},{20,24},{24,28},{28,0},{1,5},{5... | collective-permute-start | bytes 1572872 | tf_op jit(solution)/shard_map/ppermute | solution.py:12
  28.5 15.4 %collective-permute-start.1 = (f32[32,4096]{1,0:T(8,128)S(1)}, f32[32,4096]{1,0:T(8,128)S(1)}, u32[]{:S(2)}, u32[]{:S(2)}) collective-permute-start(f32[32,4096]{1,0:T(8,128)S(1)} %collective-permute-done), channel_id=1, source_target_pairs={{0,4},{4,8},{8,12},{12,16},{16,20},{20,24},{24,28},{28,0},{1,5},{5... | collective-permute-start | bytes 1572872 | tf_op jit(solution)/shard_map/ppermute | solution.py:12
  43.9 21.9 %collective-permute-start.2 = (f32[32,4096]{1,0:T(8,128)S(1)}, f32[32,4096]{1,0:T(8,128)S(1)}, u32[]{:S(2)}, u32[]{:S(2)}) collective-permute-start(f32[32,4096]{1,0:T(8,128)S(1)} %collective-permute-done.1), channel_id=1, source_target_pairs={{0,4},{4,8},{8,12},{12,16},{16,20},{20,24},{24,28},{28,0},{1,5},{5... | collective-permute-start | bytes 1572872 | tf_op jit(solution)/shard_map/ppermute | solution.py:12
  65.8 34.5 %collective-permute-start.3 = (f32[32,4096]{1,0:T(8,128)S(1)}, f32[32,4096]{1,0:T(8,128)S(1)}, u32[]{:S(2)}, u32[]{:S(2)}) collective-permute-start(f32[32,4096]{1,0:T(8,128)S(1)} %collective-permute-done.2), channel_id=1, source_target_pairs={{0,4},{4,8},{8,12},{12,16},{16,20},{20,24},{24,28},{28,0},{1,5},{5... | collective-permute-start | bytes 1572872 | tf_op jit(solution)/shard_map/ppermute | solution.py:12
  74.9 12.8 %collective-permute-start.4 = (f32[32]{0:T(128)S(1)}, f32[32]{0:T(128)S(1)}, u32[]{:S(2)}, u32[]{:S(2)}) collective-permute-start(f32[32]{0:T(128)S(1)} %get-tuple-element.137), channel_id=1, source_target_pairs={{0,4},{4,8},{8,12},{12,16},{16,20},{20,24},{24,28},{28,0},{1,5},{5... | collective-permute-start | bytes 392 | tf_op jit(solution)/shard_map/ppermute | solution.py:12
  87.7 6.3 %collective-permute-start.5 = (f32[32]{0:T(128)S(1)}, f32[32]{0:T(128)S(1)}, u32[]{:S(2)}, u32[]{:S(2)}) collective-permute-start(f32[32]{0:T(128)S(1)} %collective-permute-done.4), channel_id=1, source_target_pairs={{0,4},{4,8},{8,12},{12,16},{16,20},{20,24},{24,28},{28,0},{1,5},{5... | collective-permute-start | bytes 392 | tf_op jit(solution)/shard_map/ppermute | solution.py:12
  94.0 6.3 %collective-permute-start.6 = (f32[32]{0:T(128)S(1)}, f32[32]{0:T(128)S(1)}, u32[]{:S(2)}, u32[]{:S(2)}) collective-permute-start(f32[32]{0:T(128)S(1)} %collective-permute-done.5), channel_id=1, source_target_pairs={{0,4},{4,8},{8,12},{12,16},{16,20},{20,24},{24,28},{28,0},{1,5},{5... | collective-permute-start | bytes 392 | tf_op jit(solution)/shard_map/ppermute | solution.py:12
  100.3 113.2 %collective-permute-start.7 = (f32[32]{0:T(128)S(1)}, f32[32]{0:T(128)S(1)}, u32[]{:S(2)}, u32[]{:S(2)}) collective-permute-start(f32[32]{0:T(128)S(1)} %collective-permute-done.6), channel_id=1, source_target_pairs={{0,4},{4,8},{8,12},{12,16},{16,20},{20,24},{24,28},{28,0},{1,5},{5... | collective-permute-start | bytes 392 | tf_op jit(solution)/shard_map/ppermute | solution.py:12
Sparse Core Ops, SparseCore 0:
  9.5 57.9 all-gather.2
  213.6 21.2 reduce-scatter.3
